TPU v7x, 32 devices: a whole 2x2x4 slice. The times are simulated.
32 devices in a mesh: ctx: 16 (over z, y, x), head: 2 (over core).
Axes of the slice: x: 2, y: 2, z: 4, core: 2. Of those that a mesh axis runs over, the one named last changes fastest.
Arguments:
- queries: float32 [8192, 512], P('ctx', 'head'), may hold values from -1024 to 1024
- keys: float32 [8192, 128], P('ctx'), may hold values from -1024 to 1024
- values: float32 [8192, 128], P('ctx'), may hold values from -6 to 6
- cotangent: float32 [8192, 512], P('ctx', 'head'), may hold values from -384 to 384
- source_ids: int32 [8192], P('ctx'), may hold values from 0 to 63
- source_weights: float32 [64], replicated, may hold values from 0.25 to 4
- q_feature: float32 [4, 128, 128], P('head'), may hold values from -4 to 4
- k_feature: float32 [128, 128], replicated, may hold values from -4 to 4
Outputs:
- grad_queries: float32 [8192, 512], P('ctx', 'head')
- grad_keys: float32 [8192, 128], P(('ctx', 'head'))
- grad_values: float32 [8192, 128], P(('ctx', 'head'))
- grad_q_feature: float32 [4, 128, 128], P('head')
- grad_k_feature: float32 [128, 128], replicated
All inputs are finite; a program needn't handle non-finite values.
Results may differ from a plain program's by a relative error of at most 0.0015.
Values sent between devices are 32-bit elements; how exact they have to be, the bound alone decides.
No kernel may reach another device: no remote copies, remote signals or barrier semaphores. Data moves between devices by JAX's collectives and lax.ppermute only.
A program may use at most 64 MiB of HBM per device.

v0:
```python
import jax
import jax.numpy as jnp
from jax import lax
from jax.sharding import PartitionSpec as P


def entering(value, axis, join, neutral, backward):
    count, mine = (lax.axis_size(axis), lax.axis_index(axis))
    pieces = jax.tree.map(lambda part: lax.all_gather(part, axis), value)
    if backward:
        pieces = jax.tree.map(lambda part: part[::-1], pieces)
        mine = count - 1 - mine
    total = jax.tree.map(
        lambda part, zero: jnp.full_like(part, 0) + jnp.asarray(zero, part.dtype), value, neutral
    )

    def turn(position, total):
        longer = join(total, jax.tree.map(lambda part: part[position], pieces))
        return jax.tree.map(lambda new, old: jnp.where(position < mine, new, old), longer, total)

    return lax.fori_loop(0, count - 1, turn, total)


def matmul(left, right):
    return jnp.dot(left, right, precision=lax.Precision.HIGHEST, preferred_element_type=jnp.float32)


def product(form, left, right):
    return jnp.einsum(
        form, left, right, precision=lax.Precision.HIGHEST, preferred_element_type=jnp.float32
    )


def feature_map(inputs, weight):
    logits = matmul(inputs, weight)
    upper = jax.nn.softmax(logits, axis=-1)
    lower = jax.nn.softmax(-logits, axis=-1)
    return (jnp.concatenate([upper, lower], axis=-1), upper, lower)


def feature_back(inputs, weight, upper, lower, grad_feat):
    half = upper.shape[-1]
    grad_upper = grad_feat[:, :half]
    grad_lower = grad_feat[:, half:]
    grad_logits = upper * (grad_upper - jnp.sum(upper * grad_upper, axis=-1, keepdims=True))
    grad_logits = grad_logits - lower * (
        grad_lower - jnp.sum(lower * grad_lower, axis=-1, keepdims=True)
    )
    return (matmul(grad_logits, weight.T), matmul(inputs.T, grad_logits))


def causal_mask(count):
    row_index = lax.broadcasted_iota(jnp.int32, (count, count), 0)
    col_index = lax.broadcasted_iota(jnp.int32, (count, count), 1)
    return (row_index >= col_index).astype(jnp.float32)


def add_pair(earlier, later):
    return (earlier[0] + later[0], earlier[1] + later[1])


def block_terms(query_c, key_c, value_c, scaled_c, prefix, prefix_tot):
    lower_mask = causal_mask(query_c.shape[1])
    scores = product("ncf,ndf->ncd", query_c, key_c) * lower_mask
    numerator = product("ncd,nde->nce", scores, value_c) + product("ncf,nfe->nce", query_c, prefix)
    normalizer = jnp.sum(scores, axis=2) + product("ncf,nf->nc", query_c, prefix_tot)
    output = numerator / normalizer[..., None]
    grad_numer = scaled_c / normalizer[..., None]
    grad_norm = -jnp.sum(scaled_c * output, axis=2) / normalizer
    grad_scores = (product("nce,nde->ncd", grad_numer, value_c) + grad_norm[..., None]) * lower_mask
    grad_query = (
        product("ncd,ndf->ncf", grad_scores, key_c)
        + product("nce,nfe->ncf", grad_numer, prefix)
        + grad_norm[..., None] * prefix_tot[:, None, :]
    )
    grad_key = product("ncd,ncf->ndf", grad_scores, query_c)
    grad_value = product("ncd,nce->nde", scores, grad_numer)
    carried = product("ncf,nce->nfe", query_c, grad_numer)
    carried_totals = product("nc,ncf->nf", grad_norm, query_c)
    return (grad_query, grad_key, grad_value, carried, carried_totals)


def on_device(queries, keys, values, cotangent, source_ids, source_weights, q_feature, k_feature):
    head_count = q_feature.shape[0]
    width = q_feature.shape[1]
    features = 2 * q_feature.shape[2]
    rows = queries.shape[0]
    piece = min(128, rows)
    pieces = rows // piece
    source_index = lax.broadcasted_iota(jnp.int32, (1, source_weights.shape[0]), 1)
    lookup = (source_ids[:, None] == source_index).astype(jnp.float32)
    weight = jnp.sum(lookup * source_weights[None, :], axis=1)
    key_feat, key_upper, key_lower = feature_map(keys, k_feature)
    key_c = key_feat.reshape(pieces, piece, features)
    value_c = values.reshape(pieces, piece, width)
    piece_state = product("ncf,nce->nfe", key_c, value_c)
    piece_tot = jnp.sum(key_c, axis=1)
    share = features // lax.axis_size("head")
    offset = lax.axis_index("head") * share
    slab_feat = lax.dynamic_slice_in_dim(key_feat, offset, share, 1)
    slab_local = (
        lax.dynamic_slice_in_dim(jnp.sum(piece_state, axis=0), offset, share, 0),
        lax.dynamic_slice_in_dim(jnp.sum(piece_tot, axis=0), offset, share, 0),
    )
    slab_zero = (jnp.zeros((share, width), jnp.float32), jnp.zeros((share,), jnp.float32))
    slab_before = entering(slab_local, "ctx", add_pair, slab_zero, False)
    earlier, earlier_totals = (
        lax.all_gather(slab_before[0], "head", axis=0, tiled=True),
        lax.all_gather(slab_before[1], "head", axis=0, tiled=True),
    )
    prefix = jnp.cumsum(piece_state, axis=0) - piece_state + earlier[None]
    prefix_tot = jnp.cumsum(piece_tot, axis=0) - piece_tot + earlier_totals[None]
    grad_keyfeat = jnp.zeros(key_feat.shape, jnp.float32)
    grad_vals = jnp.zeros(values.shape, jnp.float32)
    piece_carried = jnp.zeros((pieces, features, width), jnp.float32)
    piece_carried_tot = jnp.zeros((pieces, features), jnp.float32)
    query_grads = []
    weight_grads = []
    for head in range(head_count):
        query_head = queries[:, head * width : (head + 1) * width]
        query_feat, query_upper, query_lower = feature_map(query_head, q_feature[head])
        scaled = cotangent[:, head * width : (head + 1) * width] * weight[:, None]
        grad_query, grad_key, grad_value, carried, carried_totals = block_terms(
            query_feat.reshape(pieces, piece, features),
            key_c,
            value_c,
            scaled.reshape(pieces, piece, width),
            prefix,
            prefix_tot,
        )
        grad_head, grad_weight = feature_back(
            query_head,
            q_feature[head],
            query_upper,
            query_lower,
            grad_query.reshape(rows, features),
        )
        query_grads.append(grad_head)
        weight_grads.append(grad_weight)
        grad_keyfeat = grad_keyfeat + grad_key.reshape(rows, features)
        grad_vals = grad_vals + grad_value.reshape(rows, width)
        piece_carried = piece_carried + carried
        piece_carried_tot = piece_carried_tot + carried_totals
    carried_all = jnp.sum(piece_carried, axis=0)
    carried_tot = jnp.sum(piece_carried_tot, axis=0)
    inner_later = carried_all[None] - jnp.cumsum(piece_carried, axis=0)
    inner_tot = carried_tot[None] - jnp.cumsum(piece_carried_tot, axis=0)
    grad_keyfeat = grad_keyfeat + (
        product("nce,nfe->ncf", value_c, inner_later) + inner_tot[:, None, :]
    ).reshape(rows, features)
    grad_vals = grad_vals + product("ncf,nfe->nce", key_c, inner_later).reshape(rows, width)
    folded, folded_tot = (
        lax.psum_scatter(carried_all, "head", scatter_dimension=0, tiled=True),
        lax.psum_scatter(carried_tot, "head", scatter_dimension=0, tiled=True),
    )
    later, later_tot = entering((folded, folded_tot), "ctx", add_pair, slab_zero, True)
    slab_grad = matmul(values, later.T) + later_tot[None, :]
    current = lax.dynamic_slice_in_dim(grad_keyfeat, offset, share, 1)
    grad_keyfeat = lax.dynamic_update_slice_in_dim(grad_keyfeat, current + slab_grad, offset, 1)
    grad_vals = grad_vals + matmul(slab_feat, later)
    grad_key_part, grad_kweight = feature_back(keys, k_feature, key_upper, key_lower, grad_keyfeat)
    grad_keys, grad_values = (
        lax.psum_scatter(grad_key_part, "head", scatter_dimension=0, tiled=True),
        lax.psum_scatter(grad_vals, "head", scatter_dimension=0, tiled=True),
    )
    grad_qweight = lax.psum(jnp.stack(weight_grads, axis=0), "ctx")
    grad_kweight = lax.psum(grad_kweight, ("ctx", "head"))
    return (
        jnp.concatenate(query_grads, axis=1),
        grad_keys,
        grad_values,
        grad_qweight,
        grad_kweight,
    )


def solution(mesh):
    placed = (
        P("ctx", "head"),
        P("ctx", None),
        P("ctx", None),
        P("ctx", "head"),
        P("ctx"),
        P(),
        P("head", None, None),
        P(),
    )
    return jax.shard_map(
        on_device,
        mesh=mesh,
        in_specs=placed,
        out_specs=(
            P("ctx", "head"),
            P(("ctx", "head"), None),
            P(("ctx", "head"), None),
            P("head", None, None),
            P(),
        ),
        check_vma=False,
    )
```

profile of v0, /device:TPU:0, one launch (start us, length us, event | category | flops | bytes accessed | tf_op | source)
XLA Modules:
  0.0 441.5 jit_solution(6858536777643410984)
XLA Ops:
  7.2 1.4 fusion.102
  16.1 42.4 %all-gather.4 = f32[16,1,128]{2,1,0:T(1,128)S(1)} all-gather(f32[1,1,128]{2,1,0:T(1,128)S(1)} %dynamic-slice_bitcast_fusion.1), channel_id=3, replica_groups=mesh['ctx'=16,'head'=2] {'ctx'}, dimensions={0}, use_global_device_ids=true | all-gather | bytes 8704 | tf_op jit(solution)/shard_map/all_gather | solution.py:9
  59.9 1.8 fusion.107
  61.7 1.8 fusion.109
  63.4 5.7 %all-gather.10.cloned.1.call-done = f32[2048,128]{1,0:T(8,128)} async-done(((f32[128,128]{1,0:T(8,128)}), f32[2048,128]{1,0:T(8,128)}) %all-gather.10.cloned.1.call-update) | async-done | bytes 1048592 | tf_op jit(solution)/shard_map/all_gather | solution.py:9
  69.2 13.6 %while.32 = (s32[]{:T(128)}, f32[128,128]{1,0:T(8,128)S(1)}, f32[128]{0:T(128)S(1)}, s32[]{:T(128)}, f32[16,128,128]{2,1,0:T(8,128)}, /*index=5*/f32[16,128]{1,0:T(8,128)S(1)}, s32[]{:T(128)}, s32[]{:T(128)}) while((s32[]{:T(128)}, f32[128,128]{1,0:T(8,128)S(1)}, f32[128]{0:T(128)S(1)}, s32[]{:T(128)}, ...), condition=%wide.region_15.16_spmd.clone, body=%wide.region_14.15_spmd.clone.sunk | while | flops 49540 | bytes 198267 | solution.py:21
  82.8 1.8 all-gather.5
  86.8 2.1 all_gather.35
  94.4 1.4 fusion.33
  95.9 1.4 fusion.36
  100.2 2.5 all-reduce
  108.9 2.1 fusion.110
  112.3 1.4 fusion.2
  113.7 3.9 reduce-scatter.4.cloned.1.call-done
  117.8 41.0 %all-gather.6 = f32[16,1,128]{2,1,0:T(1,128)S(1)} all-gather(f32[1,1,128]{2,1,0:T(1,128)S(1)} %dynamic-slice_bitcast_fusion), channel_id=5, replica_groups=mesh['ctx'=16,'head'=2] {'ctx'}, dimensions={0}, use_global_device_ids=true | all-gather | bytes 8704 | tf_op jit(solution)/shard_map/all_gather | solution.py:9
  158.8 1.8 copy.212
  163.7 1.8 copy.211
  173.0 3.7 all-gather.12.cloned.1.call-done
  187.8 99.0 %all-reduce.4.cloned.1.call-done = f32[2,128,128]{1,2,0:T(8,128)} async-done(((f32[2,128,128]{1,2,0:T(8,128)}), f32[2,128,128]{1,2,0:T(8,128)}) %all-reduce.4.cloned.1.call-update) | async-done | bytes 131088 | tf_op jit(solution)/shard_map/psum | solution.py:166
  286.8 1.7 copy.181
  288.4 122.9 %all-reduce.6.cloned.1.call-done = f32[128,128]{0,1:T(8,128)} async-done(((f32[128,128]{0,1:T(8,128)}), f32[128,128]{0,1:T(8,128)}) %all-reduce.6.cloned.1.call-update) | async-done | bytes 65552 | tf_op jit(solution)/shard_map/psum | solution.py:167
  411.3 1.6 copy.182
  412.8 10.1 %reduce-scatter.8.cloned.1.call-done = f32[256,128]{1,0:T(8,128)} async-done(((f32[512,128]{1,0:T(8,128)}), f32[256,128]{1,0:T(8,128)}) %reduce-scatter.8.cloned.1.call-update) | async-done | bytes 131088 | tf_op jit(solution)/shard_map/reduce_scatter | solution.py:164
  422.9 11.7 %reduce-scatter.6.cloned.1.call-done = f32[256,128]{1,0:T(8,128)} async-done(((f32[512,128]{1,0:T(8,128)}), f32[256,128]{1,0:T(8,128)}) %reduce-scatter.6.cloned.1.call-update) | async-done | bytes 131088 | tf_op jit(solution)/shard_map/reduce_scatter | solution.py:163
  (237 shorter events, 61.3 us)
Async XLA Ops:
  7.2 1.8 copy-start
  7.2 62.0 %all-gather.10.cloned.1.call-start = ((), (), s32[]{:S(2)}) async-start(), calls=%async_computation.8 | async-start | bytes 1114112 | tf_op jit(solution)/shard_map/all_gather | solution.py:9
  9.0 2.0 copy-start.29
  10.3 107.3 %reduce-scatter.4.cloned.1.call-start = ((), (), s32[]{:S(2)}) async-start(), calls=%async_computation.3 | async-start | bytes 196608 | tf_op jit(solution)/shard_map/reduce_scatter | solution.py:153
  13.1 45.4 %copy-start.12 = (f32[512,256]{1,0:T(8,128)S(1)}, f32[512,256]{1,0:T(8,128)}, u32[]{:S(2)}) copy-start(f32[512,256]{1,0:T(8,128)} %param.12) | copy-start | bytes 1572868
  13.5 45.1 %copy-start.27 = (f32[2,128,128]{2,1,0:T(8,128)S(1)}, f32[2,128,128]{2,1,0:T(8,128)}, u32[]{:S(2)}) copy-start(f32[2,128,128]{2,1,0:T(8,128)} %param.18) | copy-start | bytes 393220
  58.6 3.1 copy-start.24
  69.2 15.4 %copy-start.15 = (f32[4,256]{0,1:T(8,128)S(1)}, f32[4,256]{0,1:T(8,128)}, u32[]{:S(2)}) copy-start(f32[4,256]{0,1:T(8,128)} %copy-done.14) | copy-start | bytes 12292
  90.0 1.8 copy-start.16
  90.0 1.8 copy-start.31
  91.8 4.1 copy-start.33
  95.9 2.1 copy-start.1
  95.9 2.1 copy-start.20
  105.7 1.3 copy-start.17
  105.7 1.3 copy-start.34
  111.0 65.7 %all-gather.12.cloned.1.call-start = ((), (), s32[]{:S(2)}) async-start(), calls=%async_computation.9 | async-start | bytes 1114112 | tf_op jit(solution)/shard_map/all_gather | solution.py:9
  111.1 1.2 copy-start.9
  117.6 169.1 %all-reduce.4.cloned.1.call-start = ((), (), s32[]{:S(2)}) async-start(), calls=%async_computation.6 | async-start | bytes 262144 | tf_op jit(solution)/shard_map/psum | solution.py:166
  158.8 1.9 copy-start.22
  173.0 238.3 %all-reduce.6.cloned.1.call-start = ((), (), s32[]{:S(2)}) async-start(), calls=%async_computation.7 | async-start | bytes 131072 | tf_op jit(solution)/shard_map/psum | solution.py:167
  176.7 1.3 copy-start.35
  181.5 241.4 %reduce-scatter.8.cloned.1.call-start = ((), (), s32[]{:S(2)}) async-start(), calls=%async_computation.5 | async-start | bytes 393216 | tf_op jit(solution)/shard_map/reduce_scatter | solution.py:164
  182.9 251.7 %reduce-scatter.6.cloned.1.call-start = ((), (), s32[]{:S(2)}) async-start(), calls=%async_computation.4 | async-start | bytes 393216 | tf_op jit(solution)/shard_map/reduce_scatter | solution.py:163
  183.7 1.3 copy-start.28
  (24 other events, 22.6 us)
Sparse Core Ops, SparseCore 0:
  11.3 57.8 all-gather.9
  111.1 6.4 reduce-scatter.3
  120.4 56.2 all-gather.11
  182.6 104.1 all-reduce.3
  292.8 118.4 all-reduce.5
  413.9 8.9 reduce-scatter.7
  425.7 8.8 reduce-scatter.5
where the time goes:
time: 443 us; the launch traced here: 441 us
  waiting for transfers between devices  257 us (58%)
  blocking collectives  89.8 us (20%)
  matrix products  32.6 us (7%)
  local copies, waits for them, and re-layouts  26.5 us (6%)
  other arithmetic  19 us (4%)
  between operations  15.4 us (3%)
    psum x1, waiting for transfers between devices, on_device(): grad_kweight = lax.psum(grad_kweight, ('ctx', 'head'))  123 us
    psum x1, waiting for transfers between devices, on_device(): grad_qweight = lax.psum(jnp.stack(weight_grads, axis=0), 'ctx')  99 us
    all_gather x2, blocking collectives, entering(): pieces = jax.tree.map(lambda part: lax.all_gather(part, axis), value)  83.5 us
    dot_general x25, matrix products, product(): jnp.einsum(form, left, right, precision=lax.Precision.HIGHEST, preferred_...  24.8 us
    unnamed x92, local copies, waits for them, and re-layouts  19.6 us
    select_n x60, other arithmetic, turn(): jnp.where(position < mine, new, old)  13.7 us
    reduce_scatter x1, waiting for transfers between devices, on_device(): lax.psum_scatter(grad_key_part, 'head', scatter_dimension=0, tiled=True)  11.7 us
    reduce_scatter x1, waiting for transfers between devices, on_device(): lax.psum_scatter(grad_vals, 'head', scatter_dimension=0, tiled=True)  10.1 us
  transfers between devices with their start and end apart: 7, of which 7 were waited for; matrix products, arithmetic and copies ran while one was open for 8% of the time, Pallas kernels for 0%

commit v1 on v0

--- a/solution.py
+++ b/solution.py
@@ -164,7 +164,8 @@
         lax.psum_scatter(grad_vals, "head", scatter_dimension=0, tiled=True),
     )
     grad_qweight = lax.psum(jnp.stack(weight_grads, axis=0), "ctx")
-    grad_kweight = lax.psum(grad_kweight, ("ctx", "head"))
+    lay_pages = lambda vector: jax.lax.all_gather(vector, ("ctx", "head")).sum(axis=0)
+    grad_kweight = lay_pages(grad_kweight)
     return (
         jnp.concatenate(query_grads, axis=1),
         grad_keys,

time: 443 us -> 399 us (0.901)
  waiting for transfers between devices: 257 us -> 204 us
  other arithmetic: 19 us -> 33.9 us
  local copies, waits for them, and re-layouts: 26.5 us -> 20.5 us
    psum x1 -> x0, waiting for transfers between devices: 123 us -> none  [on_device(): grad_kweight = lax.psum(grad_kweight, ('ctx', 'head'))]
    all_gather x0 -> x1, waiting for transfers between devices: none -> 57.2 us  [on_device(): jax.lax.all_gather(vector, ('ctx', 'head')).sum(axis=0)]
    all_gather x2, waiting for transfers between devices: 9.41 us -> 43.8 us  [entering(): pieces = jax.tree.map(lambda part: lax.all_gather(part, axis), value)]
    psum x1, waiting for transfers between devices: 99 us -> 84.3 us  [on_device(): grad_qweight = lax.psum(jnp.stack(weight_grads, axis=0), 'ctx')]
    select_n x60, other arithmetic: 13.7 us -> 26.5 us  [turn(): jnp.where(position < mine, new, old)]
    unnamed x92 -> x81, local copies, waits for them, and re-layouts: 19.6 us -> 12.5 us
  transfers between devices with their start and end apart: 7 -> 7, of which waited for: 7 -> 6; matrix products, arithmetic and copies ran while one was open for 8% -> 14% of each run, Pallas kernels for 0% -> 0%
where the time goes in v1:
time: 399 us; the launch traced here: 397 us
  waiting for transfers between devices  204 us (51%)
  blocking collectives  87.3 us (22%)
  matrix products  34.7 us (9%)
  other arithmetic  33.9 us (8%)
  local copies, waits for them, and re-layouts  20.5 us (5%)
  between operations  15.5 us (4%)
    psum x1, waiting for transfers between devices, on_device(): grad_qweight = lax.psum(jnp.stack(weight_grads, axis=0), 'ctx')  84.3 us
    all_gather x2, blocking collectives, entering(): pieces = jax.tree.map(lambda part: lax.all_gather(part, axis), value)  80.9 us
    all_gather x1, waiting for transfers between devices, on_device(): jax.lax.all_gather(vector, ('ctx', 'head')).sum(axis=0)  57.2 us
    all_gather x2, waiting for transfers between devices, entering(): pieces = jax.tree.map(lambda part: lax.all_gather(part, axis), value)  43.8 us
    select_n x60, other arithmetic, turn(): jnp.where(position < mine, new, old)  26.5 us
    dot_general x25, matrix products, product(): jnp.einsum(form, left, right, precision=lax.Precision.HIGHEST, preferred_...  25.1 us
    unnamed x81, local copies, waits for them, and re-layouts  12.5 us
    reduce_scatter x1, waiting for transfers between devices, on_device(): lax.psum_scatter(grad_key_part, 'head', scatter_dimension=0, tiled=True)  11.7 us
  transfers between devices with their start and end apart: 7, of which 6 were waited for; matrix products, arithmetic and copies ran while one was open for 14% of the time, Pallas kernels for 0%

profile of v1, /device:TPU:0, one launch (start us, length us, event | category | flops | bytes accessed | tf_op | source)
XLA Modules:
  0.0 396.6 jit_solution(15787334463513923808)
XLA Ops:
  15.5 42.4 %all-gather.5 = f32[16,1,128]{2,1,0:T(1,128)S(1)} all-gather(f32[1,1,128]{2,1,0:T(1,128)S(1)} %dynamic-slice_bitcast_fusion.1), channel_id=3, replica_groups=mesh['ctx'=16,'head'=2] {'ctx'}, dimensions={0}, use_global_device_ids=true | all-gather | bytes 8704 | tf_op jit(solution)/shard_map/all_gather | solution.py:9
  60.9 1.8 fusion.107
  62.7 1.8 fusion.109
  64.5 4.7 %all-gather.12.cloned.1.call-done = f32[2048,128]{1,0:T(8,128)} async-done(((f32[128,128]{1,0:T(8,128)}), f32[2048,128]{1,0:T(8,128)}) %all-gather.12.cloned.1.call-update) | async-done | bytes 1048592 | tf_op jit(solution)/shard_map/all_gather | solution.py:9
  69.2 13.6 %while.32 = (s32[]{:T(128)}, f32[128,128]{1,0:T(8,128)S(1)}, f32[128]{0:T(128)S(1)}, s32[]{:T(128)}, f32[16,128,128]{2,1,0:T(8,128)}, /*index=5*/f32[16,128]{1,0:T(8,128)S(1)}, s32[]{:T(128)}, s32[]{:T(128)}) while((s32[]{:T(128)}, f32[128,128]{1,0:T(8,128)S(1)}, f32[128]{0:T(128)S(1)}, s32[]{:T(128)}, ...), condition=%wide.region_15.16_spmd.clone, body=%wide.region_14.15_spmd.clone.sunk | while | flops 49540 | bytes 198267 | solution.py:21
  82.7 1.8 all-gather.6
  86.8 2.1 all_gather.41
  96.5 2.5 all-reduce
  104.7 38.5 %all-gather.7 = f32[16,1,128]{2,1,0:T(1,128)S(1)} all-gather(f32[1,1,128]{2,1,0:T(1,128)S(1)} %dynamic-slice_bitcast_fusion), channel_id=5, replica_groups=mesh['ctx'=16,'head'=2] {'ctx'}, dimensions={0}, use_global_device_ids=true | all-gather | bytes 8704 | tf_op jit(solution)/shard_map/all_gather | solution.py:9
  143.2 1.8 copy.210
  145.9 1.8 copy.208
  148.9 1.5 fusion.45
  150.5 1.6 convolution_add_fusion.2
  154.7 1.8 copy.209
  160.7 39.1 %all-gather.14.cloned.1.call-done = f32[2048,128]{1,0:T(8,128)} async-done(((f32[128,128]{1,0:T(8,128)}), f32[2048,128]{1,0:T(8,128)}) %all-gather.14.cloned.1.call-update) | async-done | bytes 1048592 | tf_op jit(solution)/shard_map/all_gather | solution.py:9
  199.8 2.4 rev.6
  202.1 13.7 %while.33 = (s32[]{:T(128)}, f32[128,128]{1,0:T(8,128)S(1)}, f32[128]{0:T(128)S(1)}, s32[]{:T(128)}, f32[16,128,128]{2,1,0:T(8,128)}, /*index=5*/f32[16,128]{1,0:T(8,128)S(1)}, s32[]{:T(128)}, s32[]{:T(128)}) while((s32[]{:T(128)}, f32[128,128]{1,0:T(8,128)S(1)}, f32[128]{0:T(128)S(1)}, s32[]{:T(128)}, ...), condition=%wide.region_35.36_spmd.clone, body=%wide.region_34.35_spmd.clone.sunk | while | flops 49540 | bytes 198267 | solution.py:21
  217.6 1.6 fusion.100
  225.6 84.3 %all-reduce.3.cloned.1.call-done = f32[2,128,128]{1,2,0:T(8,128)} async-done(((f32[2,128,128]{1,2,0:T(8,128)}), f32[2,128,128]{1,2,0:T(8,128)}) %all-reduce.3.cloned.1.call-update) | async-done | bytes 131088 | tf_op jit(solution)/shard_map/psum | solution.py:166
  309.9 1.7 copy.179
  311.6 57.2 %all-gather.16.cloned.1.call-done = f32[4096,128]{0,1:T(8,128)} async-done(((f32[128,128]{0,1:T(8,128)}), f32[4096,128]{0,1:T(8,128)}) %all-gather.16.cloned.1.call-update) | async-done | bytes 2097168 | tf_op jit(solution)/shard_map/all_gather | solution.py:167
  368.8 2.0 copy.215
  371.8 6.4 %reduce-scatter.8.cloned.1.call-done = f32[256,128]{1,0:T(8,128)} async-done(((f32[512,128]{1,0:T(8,128)}), f32[256,128]{1,0:T(8,128)}) %reduce-scatter.8.cloned.1.call-update) | async-done | bytes 131088 | tf_op jit(solution)/shard_map/reduce_scatter | solution.py:164
  378.1 11.7 %reduce-scatter.6.cloned.1.call-done = f32[256,128]{1,0:T(8,128)} async-done(((f32[512,128]{1,0:T(8,128)}), f32[256,128]{1,0:T(8,128)}) %reduce-scatter.6.cloned.1.call-update) | async-done | bytes 131088 | tf_op jit(solution)/shard_map/reduce_scatter | solution.py:163
  (227 shorter events, 70.1 us)
Async XLA Ops:
  7.2 62.0 %all-gather.12.cloned.1.call-start = ((), (), s32[]{:S(2)}) async-start(), calls=%async_computation.7 | async-start | bytes 1114112 | tf_op jit(solution)/shard_map/all_gather | solution.py:9
  10.3 3.9 copy-start.34
  10.3 138.3 %reduce-scatter.4.cloned.1.call-start = ((), (), s32[]{:S(2)}) async-start(), calls=%async_computation.3 | async-start | bytes 196608 | tf_op jit(solution)/shard_map/reduce_scatter | solution.py:153
  10.5 47.5 %copy-start.10 = (f32[512,256]{1,0:T(8,128)S(1)}, f32[512,256]{1,0:T(8,128)}, u32[]{:S(2)}) copy-start(f32[512,256]{1,0:T(8,128)} %param.12) | copy-start | bytes 1572868
  14.0 46.7 %copy-start.12 = (f32[4,256]{0,1:T(8,128)}, f32[4,256]{0,1:T(8,128)S(1)}, u32[]{:S(2)}) copy-start(f32[4,256]{0,1:T(8,128)S(1)} %reduce_sum.213) | copy-start | bytes 12292
  60.9 23.6 %copy-start.13 = (f32[4,256]{0,1:T(8,128)S(1)}, f32[4,256]{0,1:T(8,128)}, u32[]{:S(2)}) copy-start(f32[4,256]{0,1:T(8,128)} %copy-done.12) | copy-start | bytes 12292
  92.2 6.8 %copy-start.14 = (f32[4,128,128]{1,2,0:T(8,128)}, f32[4,128,128]{1,2,0:T(8,128)S(1)}, u32[]{:S(2)}) copy-start(f32[4,128,128]{1,2,0:T(8,128)S(1)} %fusion.10) | copy-start | bytes 786436
  92.7 3.2 copy-start.27
  94.1 5.4 %copy-start.2 = (f32[4,128,128]{1,2,0:T(8,128)S(1)}, f32[4,128,128]{1,2,0:T(8,128)}, u32[]{:S(2)}) copy-start(f32[4,128,128]{1,2,0:T(8,128)} %copy.155) | copy-start | bytes 786436
  102.4 42.6 %copy-start.22 = (f32[512,128]{1,0:T(8,128)S(1)}, f32[512,128]{1,0:T(8,128)}, u32[]{:S(2)}) copy-start(f32[512,128]{1,0:T(8,128)} %get-tuple-element.336) | copy-start | bytes 786436
  104.6 95.2 %all-gather.14.cloned.1.call-start = ((), (), s32[]{:S(2)}) async-start(), calls=%async_computation.8 | async-start | bytes 1114112 | tf_op jit(solution)/shard_map/all_gather | solution.py:9
  148.7 161.3 %all-reduce.3.cloned.1.call-start = ((), (), s32[]{:S(2)}) async-start(), calls=%async_computation.6 | async-start | bytes 262144 | tf_op jit(solution)/shard_map/psum | solution.py:166
  159.4 42.8 %copy-start.29 = (f32[128]{0:T(128)S(1)}, f32[128]{0:T(128)}, u32[]{:S(2)}) copy-start(f32[128]{0:T(128)} %custom-call.3) | copy-start | bytes 1540
  159.5 42.6 %copy-start.6 = (f32[512,128]{0,1:T(8,128)}, f32[512,128]{0,1:T(8,128)S(1)}, u32[]{:S(2)}) copy-start(f32[512,128]{0,1:T(8,128)S(1)} %multiply_subtract_fusion.2) | copy-start | bytes 786436
  160.6 208.2 %all-gather.16.cloned.1.call-start = ((), (), s32[]{:S(2)}) async-start(), calls=%async_computation.9 | async-start | bytes 2162688 | tf_op jit(solution)/shard_map/all_gather | solution.py:167
  202.1 14.3 %copy-start.19 = (f32[512,128]{1,0:T(8,128)S(1)}, f32[512,128]{1,0:T(8,128)}, u32[]{:S(2)}) copy-start(f32[512,128]{1,0:T(8,128)} %param.13) | copy-start | bytes 786436
  216.3 4.0 copy-start.3
  216.5 3.8 copy-start.21
  217.5 160.6 %reduce-scatter.8.cloned.1.call-start = ((), (), s32[]{:S(2)}) async-start(), calls=%async_computation.5 | async-start | bytes 393216 | tf_op jit(solution)/shard_map/reduce_scatter | solution.py:164
  219.2 3.2 copy-start.5
  219.2 3.2 copy-start.24
  219.2 3.6 copy-start.25
  220.3 3.9 copy-start.7
  222.3 167.5 %reduce-scatter.6.cloned.1.call-start = ((), (), s32[]{:S(2)}) async-start(), calls=%async_computation.4 | async-start | bytes 393216 | tf_op jit(solution)/shard_map/reduce_scatter | solution.py:163
  (18 other events, 39.4 us)
Sparse Core Ops, SparseCore 0:
  11.3 57.8 all-gather.11
  104.7 6.4 reduce-scatter.3
  148.8 50.9 all-gather.13
  205.6 104.2 all-reduce.2
  313.2 55.5 all-gather.15
  371.5 6.5 reduce-scatter.7
  380.9 8.8 reduce-scatter.5
